TPU v7x, 32 devices: a whole 2x2x4 slice. The times are simulated.
32 devices in a mesh: groups: 2 (over y), tok: 16 (over z, x, core).
Axes of the slice: x: 2, y: 2, z: 4, core: 2. Of those that a mesh axis runs over, the one named last changes fastest.
Arguments:
- queries: bfloat16 [2048, 2048], P(('groups', 'tok')), parts along dimension 0, may hold values from -256 to 256, as said below
- fresh_keys: bfloat16 [2048, 2048], P(('groups', 'tok')), parts along dimension 0, may hold values from -6 to 6, as said below
- fresh_values: bfloat16 [2048, 2048], P(('groups', 'tok')), parts along dimension 0, may hold values from -6 to 6
- stale_keys: bfloat16 [2048, 2048], P(('groups', 'tok')), parts along dimension 0, may hold values from -6 to 6
- stale_values: bfloat16 [2048, 2048], P(('groups', 'tok')), parts along dimension 0, may hold values from -6 to 6
- patch_starts: int32 [32], P('groups'), parts along dimension 0, may hold values from 0 to 1023, as said below
- order_starts: int32 [32], P('groups'), parts along dimension 0, may hold values from 0 to 1023, as said below
Outputs:
- attended: bfloat16 [2048, 2048], P(('groups', 'tok')), parts along dimension 0
There are 2 independent parts, one for each index of `groups`. A program takes and returns all parts, laid end to end along the dimension named above; each array names one. Nothing has to cross between parts.
Inputs may be any that keep to these rules, and one draw needn't show every extreme that they name: `patch_starts`: strictly increasing; the first entry is 0. `order_starts`: the entries of patch_starts, each once, in processing order. `queries`: entries are finite. `fresh_keys`: entries are finite.
All inputs are finite; a program needn't handle non-finite values.
Results may differ from a plain program's by a relative error of at most 0.0049.
Values may be sent and summed in bfloat16 or wider, within the bound.
A program may use at most 128 MiB of HBM per device.

v0:
```python
import math
import jax
import jax.numpy as jnp
from jax import lax
from jax.sharding import PartitionSpec as P

HEADS = 16
HEAD_DIM = 128


def token_ranks(positions, patch_starts, order_starts):
    patch_count = patch_starts.shape[0]
    slot_ids = jnp.arange(patch_count, dtype=jnp.int32)
    patch_of = jnp.sum((patch_starts[None, :] <= positions[:, None]).astype(jnp.int32), axis=1) - 1
    matches = (order_starts[:, None] == patch_starts[None, :]).astype(jnp.int32)
    rank_of = jnp.sum(matches * slot_ids[:, None], axis=0)
    one_hot = (patch_of[:, None] == slot_ids[None, :]).astype(jnp.int32)
    return jnp.sum(one_hot * rank_of[None, :], axis=1)


def masked_scores(query_block, query_rank, key_stack, key_rank):
    dims = (((1,), (1,)), ((), ()))
    score_scale = 1.0 / math.sqrt(query_block.shape[-1])
    fresh_scores = (
        lax.dot_general(query_block, key_stack[0], dims, preferred_element_type=jnp.float32)
        * score_scale
    )
    stale_scores = (
        lax.dot_general(query_block, key_stack[2], dims, preferred_element_type=jnp.float32)
        * score_scale
    )
    fresh_ok = key_rank[None, :] <= query_rank[:, None]
    fresh_scores = jnp.where(fresh_ok, fresh_scores, -jnp.inf)
    stale_scores = jnp.where(fresh_ok, -jnp.inf, stale_scores)
    return (fresh_scores, stale_scores)


def attend_block(query_block, query_rank, key_stack, key_rank):
    fresh_scores, stale_scores = masked_scores(query_block, query_rank, key_stack, key_rank)
    row_max = jnp.maximum(jnp.max(fresh_scores, axis=1), jnp.max(stale_scores, axis=1))[:, None]
    fresh_exp = jnp.exp(fresh_scores - row_max)
    stale_exp = jnp.exp(stale_scores - row_max)
    row_total = jnp.sum(fresh_exp, axis=1, keepdims=True) + jnp.sum(
        stale_exp, axis=1, keepdims=True
    )
    fresh_probs = (fresh_exp / row_total).astype(jnp.bfloat16)
    stale_probs = (stale_exp / row_total).astype(jnp.bfloat16)
    mixed = jnp.dot(fresh_probs, key_stack[1], preferred_element_type=jnp.float32)
    mixed = mixed + jnp.dot(stale_probs, key_stack[3], preferred_element_type=jnp.float32)
    return mixed.astype(jnp.bfloat16)


def attend_rows(query_rows, query_rank, key_stack, key_rank):
    row_count = query_rows.shape[0]
    block_rows = 512
    blocks = row_count // block_rows

    def one_block(inputs):
        return attend_block(inputs[0], inputs[1], key_stack, key_rank)

    result = lax.map(
        one_block,
        (
            query_rows.reshape(blocks, block_rows, query_rows.shape[1]),
            query_rank.reshape(blocks, block_rows),
        ),
    )
    return result.reshape(row_count, query_rows.shape[1])


def shards(queries, fresh_keys, fresh_values, stale_keys, stale_values, patch_starts, order_starts):
    devices = lax.axis_size("tok")
    tok_dev, row_width = queries.shape
    group_size = devices // HEADS
    slab_rows = tok_dev // group_size
    my_index = lax.axis_index("tok")
    member = my_index % group_size
    query_slabs = (
        queries.reshape(group_size, slab_rows, HEADS, HEAD_DIM)
        .transpose(2, 0, 1, 3)
        .reshape(devices, slab_rows, HEAD_DIM)
    )
    query_rows = lax.all_to_all(query_slabs, "tok", split_axis=0, concat_axis=0, tiled=True)
    stacked = jnp.stack([fresh_keys, fresh_values, stale_keys, stale_values]).reshape(
        4, tok_dev, HEADS, HEAD_DIM
    )
    sender_base = jnp.arange(devices, dtype=jnp.int32)[:, None] * tok_dev
    slab_offsets = jnp.arange(slab_rows, dtype=jnp.int32)[None, :]
    query_pos = (sender_base + member * slab_rows + slab_offsets).reshape(-1)
    by_head = stacked.transpose(0, 2, 1, 3)[:, :, None]
    spread = jnp.broadcast_to(by_head, (4, HEADS, group_size, tok_dev, HEAD_DIM)).reshape(
        4, devices, tok_dev, HEAD_DIM
    )
    arrived = lax.all_to_all(spread, "tok", split_axis=1, concat_axis=1, tiled=True)
    key_stack = arrived.reshape(4, devices * tok_dev, HEAD_DIM)
    key_rank = token_ranks(
        jnp.arange(devices * tok_dev, dtype=jnp.int32), patch_starts, order_starts
    )
    query_rank = token_ranks(query_pos, patch_starts, order_starts)
    attended = attend_rows(
        query_rows.reshape(devices * slab_rows, HEAD_DIM), query_rank, key_stack, key_rank
    )
    returned = lax.all_to_all(
        attended.reshape(devices, slab_rows, HEAD_DIM),
        "tok",
        split_axis=0,
        concat_axis=0,
        tiled=True,
    )
    return (
        returned.reshape(HEADS, group_size, slab_rows, HEAD_DIM)
        .transpose(1, 2, 0, 3)
        .reshape(tok_dev, row_width)
    )


def solution(mesh):
    placed = (
        P(("groups", "tok"), None),
        P(("groups", "tok"), None),
        P(("groups", "tok"), None),
        P(("groups", "tok"), None),
        P(("groups", "tok"), None),
        P("groups"),
        P("groups"),
    )
    return jax.shard_map(
        shards, mesh=mesh, in_specs=placed, out_specs=P(("groups", "tok"), None), check_vma=False
    )
```

profile of v0, /device:TPU:0, one launch (start us, length us, event | category | flops | bytes accessed | tf_op | source)
XLA Modules:
  0.0 72.3 jit_solution(15579702160136215881)
XLA Ops:
  0.0 1.0 %copy.24 = bf16[8,8,16,128]{3,2,1,0:T(8,128)(2,1)S(1)} copy(bf16[8,8,16,128]{3,1,2,0:T(8,128)(2,1)} %bitcast.87) | data formatting | bytes 524288
  1.0 1.0 %copy.25 = bf16[8,8,16,128]{3,2,1,0:T(8,128)(2,1)S(1)} copy(bf16[8,8,16,128]{3,1,2,0:T(8,128)(2,1)} %bitcast.88) | data formatting | bytes 524288
  2.0 1.0 %copy.26 = bf16[8,8,16,128]{3,2,1,0:T(8,128)(2,1)S(1)} copy(bf16[8,8,16,128]{3,1,2,0:T(8,128)(2,1)} %bitcast.89) | data formatting | bytes 524288
  3.0 1.0 %copy.27 = bf16[8,8,16,128]{3,2,1,0:T(8,128)(2,1)S(1)} copy(bf16[8,8,16,128]{3,1,2,0:T(8,128)(2,1)} %bitcast.90) | data formatting | bytes 524288
  4.0 0.1 maximum_bitcast_fusion
  4.1 0.0 copy-start
  4.1 1.3 %copy.20 = bf16[4,16,64,128]{3,2,0,1:T(8,128)(2,1)} copy(bf16[4,16,64,128]{3,1,2,0:T(8,128)(2,1)S(1)} %maximum_bitcast_fusion) | data formatting | bytes 2097152 | tf_op jit(solution)/shard_map/transpose | solution.py:90
  5.4 0.0 copy-start.1
  5.4 0.0 copy-start.2
  5.4 7.5 %all-to-all-start.1 = ((bf16[4,16,64,128]{3,2,0,1:T(8,128)(2,1)}), bf16[4,16,64,128]{3,2,0,1:T(8,128)(2,1)S(1)}, u32[]{:S(2)}, u32[]{:S(2)}) async-start(bf16[4,16,64,128]{3,2,0,1:T(8,128)(2,1)} %copy.20), calls=%async_computation.1 | async-start | bytes 2097152 | tf_op jit(solution)/shard_map/all_to_all | solution.py:94
  12.9 0.0 copy-done
  13.0 0.8 %copy.32 = bf16[1,64,16,128]{3,1,2,0:T(8,128)(2,1)} copy(bf16[1,64,16,128]{3,2,1,0:T(8,128)(2,1)S(1)} %bitcast.82) | data formatting | bytes 524288 | tf_op jit(solution)/shard_map/reshape | solution.py:79
  13.8 0.1 iota_add_fusion
  13.8 22.0 %all-to-all-done.1 = bf16[4,16,64,128]{3,2,0,1:T(8,128)(2,1)S(1)} async-done(((bf16[4,16,64,128]{3,2,0,1:T(8,128)(2,1)}), bf16[4,16,64,128]{3,2,0,1:T(8,128)(2,1)S(1)}, u32[]{:S(2)}, u32[]{:S(2)}) %all-to-all-start.1) | async-done | bytes 1048608 | tf_op jit(solution)/shard_map/all_to_all | solution.py:94
  35.8 6.8 %all-to-all-start = ((bf16[16,64,128]{2,1,0:T(8,128)(2,1)}), bf16[16,64,128]{2,1,0:T(8,128)(2,1)S(1)}, u32[]{:S(2)}, u32[]{:S(2)}) async-start(bf16[16,64,128]{2,1,0:T(8,128)(2,1)} %bitcast.62), calls=%async_computation | async-start | bytes 524288 | tf_op jit(solution)/shard_map/all_to_all | solution.py:83
  42.6 0.0 copy-done.1
  42.6 0.0 copy-done.2
  42.6 0.1 select_reduce_fusion.2
  42.7 0.1 add.53
  42.8 0.1 convert_reduce_fusion
  42.9 0.1 select_reduce_fusion
  43.0 0.1 copy.21
  43.1 9.5 %all-to-all-done = bf16[16,64,128]{2,1,0:T(8,128)(2,1)S(1)} async-done(((bf16[16,64,128]{2,1,0:T(8,128)(2,1)}), bf16[16,64,128]{2,1,0:T(8,128)(2,1)S(1)}, u32[]{:S(2)}, u32[]{:S(2)}) %all-to-all-start) | async-done | bytes 262176 | tf_op jit(solution)/shard_map/all_to_all | solution.py:83
  52.6 6.0 %while.10 = (s32[]{:T(128)}, bf16[2,512,128]{2,1,0:T(8,128)(2,1)S(1)}, s32[1024]{0:T(1024)S(1)}, s32[2,512]{1,0:T(2,128)S(1)}, bf16[2,512,128]{2,1,0:T(8,128)(2,...) while((s32[]{:T(128)}, bf16[2,512,128]{2,1,0:T(8,128)(2,1)S(1)}, s32[1024]{0:T(1024)S(1)}, ...), condition=%wide.region_10.11_spmd, body=%wide.region_5.10_spmd.sunk | while | flops 546438144 | bytes 14596189 | solution.py:61
  52.6 0.5 fusion.31
  53.2 0.5 fusion.32
  53.7 0.7 fusion.33
  54.4 0.6 fusion.34
  55.0 0.6 fusion.35
  55.7 0.5 fusion.31
  56.2 0.5 fusion.32
  56.7 0.7 fusion.33
  57.5 0.6 fusion.34
  58.0 0.6 fusion.35
  58.7 12.7 %all_to_all.15 = bf16[16,64,128]{2,1,0:T(8,128)(2,1)S(1)} all-to-all(bf16[16,64,128]{2,1,0:T(8,128)(2,1)S(1)} %bitcast.93), channel_id=1, replica_groups=mesh['groups'=2,'tok'=16] {'tok'}, dimensions={0} | all-to-all | bytes 524288 | tf_op jit(solution)/shard_map/all_to_all | solution.py:103
  71.3 0.2 copy.22
  71.5 0.8 %copy.31 = bf16[8,8,16,128]{3,1,2,0:T(8,128)(2,1)} copy(bf16[8,8,16,128]{3,2,1,0:T(8,128)(2,1)S(1)} %bitcast.81) | data formatting | bytes 524288
  (11 shorter events, 0.1 us)
Async XLA Ops:
  4.1 8.8 %copy-start = (bf16[64,2048]{1,0:T(8,128)(2,1)S(1)}, bf16[64,2048]{1,0:T(8,128)(2,1)}, u32[]{:S(2)}) copy-start(bf16[64,2048]{1,0:T(8,128)(2,1)} %param.9) | copy-start | bytes 786436
  5.4 37.2 %copy-start.1 = (s32[16]{0:T(128)S(1)}, s32[16]{0:T(128)}, u32[]{:S(2)}) copy-start(s32[16]{0:T(128)} %param.14) | copy-start | bytes 196
  5.4 37.2 %copy-start.2 = (s32[16]{0:T(128)S(1)}, s32[16]{0:T(128)}, u32[]{:S(2)}) copy-start(s32[16]{0:T(128)} %param.15) | copy-start | bytes 196
  5.4 30.4 %all-to-all-start.1 = ((bf16[4,16,64,128]{3,2,0,1:T(8,128)(2,1)}), bf16[4,16,64,128]{3,2,0,1:T(8,128)(2,1)S(1)}, u32[]{:S(2)}, u32[]{:S(2)}) async-start(bf16[4,16,64,128]{3,2,0,1:T(8,128)(2,1)} %copy.20), calls=%async_computation.1 | async-start | bytes 2097152 | tf_op jit(solution)/shard_map/all_to_all | solution.py:94
  35.8 16.8 %all-to-all-start = ((bf16[16,64,128]{2,1,0:T(8,128)(2,1)}), bf16[16,64,128]{2,1,0:T(8,128)(2,1)S(1)}, u32[]{:S(2)}, u32[]{:S(2)}) async-start(bf16[16,64,128]{2,1,0:T(8,128)(2,1)} %bitcast.62), calls=%async_computation | async-start | bytes 524288 | tf_op jit(solution)/shard_map/all_to_all | solution.py:83
where the time goes:
time: 72.7 us; the launch traced here: 72.3 us
  waiting for transfers between devices  31.5 us (43%)
  starting transfers between devices  14.3 us (20%)
  blocking collectives  12.7 us (17%)
  local copies, waits for them, and re-layouts  7.16 us (10%)
  matrix products  4.5 us (6%)
  other arithmetic  1.96 us (3%)
    all_to_all x1, waiting for transfers between devices, shards(): lax.all_to_all(spread, 'tok', split_axis=1, concat_axis=1, tiled=True)  22 us
    all_to_all x1, blocking collectives, shards(): lax.all_to_all(attended.reshape(devices, slab_rows, HEAD_DIM), 'tok', spl...  12.7 us
    all_to_all x1, waiting for transfers between devices, shards(): lax.all_to_all(query_slabs, 'tok', split_axis=0, concat_axis=0, tiled=True)  9.51 us
    all_to_all x1, starting transfers between devices, shards(): lax.all_to_all(spread, 'tok', split_axis=1, concat_axis=1, tiled=True)  7.52 us
    all_to_all x1, starting transfers between devices, shards(): lax.all_to_all(query_slabs, 'tok', split_axis=0, concat_axis=0, tiled=True)  6.79 us
    unnamed x12, local copies, waits for them, and re-layouts  4.77 us
  transfers between devices with their start and end apart: 2, of which 2 were waited for; matrix products, arithmetic and copies ran while one was open for 2% of the time, Pallas kernels for 0%

commit v1 on v0

--- a/solution.py
+++ b/solution.py
@@ -91,7 +91,9 @@
     spread = jnp.broadcast_to(by_head, (4, HEADS, group_size, tok_dev, HEAD_DIM)).reshape(
         4, devices, tok_dev, HEAD_DIM
     )
-    arrived = lax.all_to_all(spread, "tok", split_axis=1, concat_axis=1, tiled=True)
+    shards_2 = jnp.split(spread, lax.axis_size("tok"), axis=1)
+    arrived_2 = lax.all_to_all(jnp.stack(shards_2), "tok", 0, 0)
+    arrived = jnp.concatenate(arrived_2, axis=1)
     key_stack = arrived.reshape(4, devices * tok_dev, HEAD_DIM)
     key_rank = token_ranks(
         jnp.arange(devices * tok_dev, dtype=jnp.int32), patch_starts, order_starts

time: 72.7 us -> 83.8 us (1.15)
  local copies, waits for them, and re-layouts: 7.16 us -> 18.4 us
    unnamed x12 -> x27, local copies, waits for them, and re-layouts: 4.77 us -> 14.2 us
    split x0 -> x1, local copies, waits for them, and re-layouts: none -> 2.41 us  [shards(): shards_2 = jnp.split(spread, lax.axis_size('tok'), axis=1)]
    transpose x1 -> x0, local copies, waits for them, and re-layouts: 1.26 us -> none  [shards(): by_head = stacked.transpose(0, 2, 1, 3)[:, :, None]]
where the time goes in v1:
time: 83.8 us; the launch traced here: 83.4 us
  waiting for transfers between devices  31.5 us (38%)
  local copies, waits for them, and re-layouts  18.4 us (22%)
  starting transfers between devices  14.2 us (17%)
  blocking collectives  12.7 us (15%)
  matrix products  4.5 us (5%)
  other arithmetic  1.96 us (2%)
    all_to_all x1, waiting for transfers between devices, shards(): arrived_2 = lax.all_to_all(jnp.stack(shards_2), 'tok', 0, 0)  22 us
    unnamed x27, local copies, waits for them, and re-layouts  14.2 us
    all_to_all x1, blocking collectives, shards(): lax.all_to_all(attended.reshape(devices, slab_rows, HEAD_DIM), 'tok', spl...  12.7 us
    all_to_all x1, waiting for transfers between devices, shards(): lax.all_to_all(query_slabs, 'tok', split_axis=0, concat_axis=0, tiled=True)  9.51 us
    all_to_all x1, starting transfers between devices, shards(): arrived_2 = lax.all_to_all(jnp.stack(shards_2), 'tok', 0, 0)  7.39 us
    all_to_all x1, starting transfers between devices, shards(): lax.all_to_all(query_slabs, 'tok', split_axis=0, concat_axis=0, tiled=True)  6.79 us
    split x1, local copies, waits for them, and re-layouts, shards(): shards_2 = jnp.split(spread, lax.axis_size('tok'), axis=1)  2.41 us
  transfers between devices with their start and end apart: 2, of which 2 were waited for; matrix products, arithmetic and copies ran while one was open for 2% of the time, Pallas kernels for 0%

profile of v1, /device:TPU:0, one launch (start us, length us, event | category | flops | bytes accessed | tf_op | source)
XLA Modules:
  0.0 83.4 jit_solution(10716623988944800960)
XLA Ops:
  0.0 1.0 %copy.221 = bf16[8,8,16,128]{3,2,1,0:T(8,128)(2,1)S(1)} copy(bf16[8,8,16,128]{3,1,2,0:T(8,128)(2,1)} %bitcast.121) | data formatting | bytes 524288
  1.0 1.0 %copy.222 = bf16[8,8,16,128]{3,2,1,0:T(8,128)(2,1)S(1)} copy(bf16[8,8,16,128]{3,1,2,0:T(8,128)(2,1)} %bitcast.122) | data formatting | bytes 524288
  2.0 1.0 %copy.223 = bf16[8,8,16,128]{3,2,1,0:T(8,128)(2,1)S(1)} copy(bf16[8,8,16,128]{3,1,2,0:T(8,128)(2,1)} %bitcast.123) | data formatting | bytes 524288
  3.0 1.0 %copy.224 = bf16[8,8,16,128]{3,2,1,0:T(8,128)(2,1)S(1)} copy(bf16[8,8,16,128]{3,1,2,0:T(8,128)(2,1)} %bitcast.124) | data formatting | bytes 524288
  4.0 0.1 maximum_bitcast_fusion
  4.1 2.4 %fusion.22 = (bf16[4,1,64,128]{3,1,2,0:T(2,128)(2,1)S(1)}, bf16[4,1,64,128]{3,1,2,0:T(2,128)(2,1)S(1)}, bf16[4,1,64,128]{3,1,2,0:T(2,128)(2,1)S(1)}, bf16[4,1,64...) fusion(bf16[4,16,64,128]{3,1,2,0:T(8,128)(2,1)S(1)} %maximum_bi, ...), kind=kLoop, calls=%fused_computation.61 | loop fusion | bytes 2097152 | tf_op jit(solution)/shard_map/split | solution.py:94
  6.5 0.6 bitcast_dynamic-update-slice_fusion.15
  7.2 0.6 bitcast_dynamic-update-slice_fusion.14
  7.8 0.6 bitcast_dynamic-update-slice_fusion.13
  8.4 0.6 bitcast_dynamic-update-slice_fusion.12
  9.1 0.6 bitcast_dynamic-update-slice_fusion.11
  9.7 0.6 bitcast_dynamic-update-slice_fusion.10
  10.3 0.6 bitcast_dynamic-update-slice_fusion.9
  10.9 0.6 bitcast_dynamic-update-slice_fusion.8
  11.6 0.6 bitcast_dynamic-update-slice_fusion.7
  12.2 0.6 bitcast_dynamic-update-slice_fusion.6
  12.8 0.6 bitcast_dynamic-update-slice_fusion.5
  13.5 0.6 bitcast_dynamic-update-slice_fusion.4
  14.1 0.6 bitcast_dynamic-update-slice_fusion.3
  14.7 0.6 bitcast_dynamic-update-slice_fusion.2
  15.3 0.6 bitcast_dynamic-update-slice_fusion.1
  16.0 0.6 bitcast_dynamic-update-slice_fusion
  16.6 7.4 %all-to-all-start.1 = ((bf16[16,4,1,64,128]{4,3,1,2,0:T(8,128)(2,1)}), bf16[16,4,1,64,128]{4,3,1,2,0:T(8,128)(2,1)S(1)}, u32[]{:S(2)}, u32[]{:S(2)}) async-start(bf16[16,4,1,64,128]{4,3,1,2,0:T(8,128)(2,1)} %bitcast_dynamic-update-slice_fusion), calls=%async_computation.1 | async-start | bytes 2097152 | tf_op jit(solution)/shard_map/all_to_all | solution.py:95
  24.0 0.0 copy-done
  24.1 0.8 copy.245
  24.8 0.1 iota_add_fusion
  24.9 22.0 %all-to-all-done.1 = bf16[16,4,1,64,128]{4,3,1,2,0:T(8,128)(2,1)S(1)} async-done(((bf16[16,4,1,64,128]{4,3,1,2,0:T(8,128)(2,1)}), bf16[16,4,1,64,128]{4,3,1,2,0:T(8,128)(2,1)S(1)}, u32[]{:S(2)}, u32[]{:S(2)}) %all-to-all-start.1) | async-done | bytes 1048608 | tf_op jit(solution)/shard_map/all_to_all | solution.py:95
  46.9 6.8 %all-to-all-start = ((bf16[16,64,128]{2,1,0:T(8,128)(2,1)}), bf16[16,64,128]{2,1,0:T(8,128)(2,1)S(1)}, u32[]{:S(2)}, u32[]{:S(2)}) async-start(bf16[16,64,128]{2,1,0:T(8,128)(2,1)} %bitcast.96), calls=%async_computation | async-start | bytes 524288 | tf_op jit(solution)/shard_map/all_to_all | solution.py:83
  53.7 0.1 select_reduce_fusion.2
  53.8 0.1 add.53
  53.9 0.1 convert_reduce_fusion
  54.0 0.1 select_reduce_fusion
  54.1 0.1 copy.202
  54.2 9.5 %all-to-all-done = bf16[16,64,128]{2,1,0:T(8,128)(2,1)S(1)} async-done(((bf16[16,64,128]{2,1,0:T(8,128)(2,1)}), bf16[16,64,128]{2,1,0:T(8,128)(2,1)S(1)}, u32[]{:S(2)}, u32[]{:S(2)}) %all-to-all-start) | async-done | bytes 262176 | tf_op jit(solution)/shard_map/all_to_all | solution.py:83
  63.7 6.0 %while.10 = (s32[]{:T(128)}, bf16[2,512,128]{2,1,0:T(8,128)(2,1)S(1)}, s32[1024]{0:T(1024)S(1)}, s32[2,512]{1,0:T(2,128)S(1)}, bf16[2,512,128]{2,1,0:T(8,128)(2,...) while((s32[]{:T(128)}, bf16[2,512,128]{2,1,0:T(8,128)(2,1)S(1)}, s32[1024]{0:T(1024)S(1)}, ...), condition=%wide.region_10.11_spmd, body=%wide.region_5.10_spmd.sunk | while | flops 546438144 | bytes 14596189 | solution.py:61
  63.7 0.5 fusion.32
  64.3 0.5 fusion.33
  64.8 0.7 fusion.34
  65.5 0.6 fusion.35
  66.1 0.6 fusion.36
  66.7 0.5 fusion.32
  67.3 0.5 fusion.33
  67.8 0.7 fusion.34
  68.5 0.6 fusion.35
  69.1 0.6 fusion.36
  69.7 12.7 %all_to_all.15 = bf16[16,64,128]{2,1,0:T(8,128)(2,1)S(1)} all-to-all(bf16[16,64,128]{2,1,0:T(8,128)(2,1)S(1)} %bitcast.127), channel_id=1, replica_groups=mesh['groups'=2,'tok'=16] {'tok'}, dimensions={0} | all-to-all | bytes 524288 | tf_op jit(solution)/shard_map/all_to_all | solution.py:105
  82.4 0.2 copy.203
  82.6 0.8 copy.244
  (16 shorter events, 0.1 us)
Async XLA Ops:
  9.7 14.3 %copy-start = (bf16[64,2048]{1,0:T(8,128)(2,1)S(1)}, bf16[64,2048]{1,0:T(8,128)(2,1)}, u32[]{:S(2)}) copy-start(bf16[64,2048]{1,0:T(8,128)(2,1)} %param.9) | copy-start | bytes 786436
  14.7 39.0 %copy-start.1 = (s32[16]{0:T(128)S(1)}, s32[16]{0:T(128)}, u32[]{:S(2)}) copy-start(s32[16]{0:T(128)} %param.14) | copy-start | bytes 196
  14.7 39.0 %copy-start.2 = (s32[16]{0:T(128)S(1)}, s32[16]{0:T(128)}, u32[]{:S(2)}) copy-start(s32[16]{0:T(128)} %param.15) | copy-start | bytes 196
  16.6 30.3 %all-to-all-start.1 = ((bf16[16,4,1,64,128]{4,3,1,2,0:T(8,128)(2,1)}), bf16[16,4,1,64,128]{4,3,1,2,0:T(8,128)(2,1)S(1)}, u32[]{:S(2)}, u32[]{:S(2)}) async-start(bf16[16,4,1,64,128]{4,3,1,2,0:T(8,128)(2,1)} %bitcast_dynamic-update-slice_fusion), calls=%async_computation.1 | async-start | bytes 2097152 | tf_op jit(solution)/shard_map/all_to_all | solution.py:95
  46.9 16.8 %all-to-all-start = ((bf16[16,64,128]{2,1,0:T(8,128)(2,1)}), bf16[16,64,128]{2,1,0:T(8,128)(2,1)S(1)}, u32[]{:S(2)}, u32[]{:S(2)}) async-start(bf16[16,64,128]{2,1,0:T(8,128)(2,1)} %bitcast.96), calls=%async_computation | async-start | bytes 524288 | tf_op jit(solution)/shard_map/all_to_all | solution.py:83
